TPU v7x, 128 devices: a whole 4x4x4 slice. The times are simulated.
128 devices in a mesh: frame: 16 (over y, x), head: 8 (over z, core).
Axes of the slice: x: 4, y: 4, z: 4, core: 2. Of those that a mesh axis runs over, the one named last changes fastest.
Arguments:
- tokens: bfloat16 [12288, 5120], P('frame', 'head'), may hold values from -40 to 40
- mask_block_frame: int32 [96], replicated, may hold values from 0 to 7, as said below
- attended_key_blocks: int32 [96, 10], replicated, may hold values from 0 to 95, as said below
- frozen_query_key_value: bfloat16 [5120, 3, 3072], P(None, None, 'head'), may hold values from -0.104815686 to 0.104815686
- query_key_value_down_weight: bfloat16 [5120, 192], replicated, may hold values from -0.078125 to 0.078125
- query_key_value_up_weight: bfloat16 [64, 3, 3072], P(None, None, 'head'), may hold values from -0.375 to 0.375
- frozen_output_weight: bfloat16 [3072, 5120], P('head'), may hold values from -0.109375 to 0.109375
- output_down_weight: bfloat16 [3072, 64], P('head'), may hold values from -0.109375 to 0.109375
- output_up_weight: bfloat16 [64, 5120], P(None, 'head'), may hold values from -0.75 to 0.75
Outputs:
- attended_out: bfloat16 [12288, 5120], P('frame', 'head')
Inputs may be any that keep to these rules, and one draw needn't show every extreme that they name: `mask_block_frame`: Non-decreasing along the blocks; every frame from 0 to 7 holds at least one block. `attended_key_blocks`: row b lists 10 distinct key blocks and always includes b itself. Take aligned groups of 6 blocks; for a group of query blocks and another group g groups away (g >= 1), the rows of the first group together name exactly 4 // 2 ** (g - 1) distinct blocks of the second, except that a group exactly 8 groups away is named by exactly the larger of that number and 2.
All inputs are finite; a program needn't handle non-finite values.
Results may differ from a plain program's by a relative error of at most 0.017.
Values may be sent and summed in bfloat16 or wider, within the bound.
A program may use at most 128 MiB of HBM per device.

v0:
```python
import math
import jax
import jax.numpy as jnp
from jax import lax
from jax.sharding import PartitionSpec as P

MODEL_WIDTH = 5120
HEAD_SIZE = 128
BLOCK = 128


def rotate_pairs(values, frame_pos, place):
    time_pairs = (HEAD_SIZE - 4 * (HEAD_SIZE // 6)) // 2
    space_pairs = (HEAD_SIZE - 2 * time_pairs) // 2
    time_freq = 10000.0 ** (-jnp.arange(time_pairs).astype(jnp.float32) / time_pairs)
    space_freq = 10000.0 ** (-jnp.arange(space_pairs).astype(jnp.float32) / space_pairs)
    time_angle = frame_pos[:, None] * time_freq[None, :]
    space_angle = place[:, None] * space_freq[None, :]
    cos_time = jnp.cos(time_angle)[:, None, :]
    sin_time = jnp.sin(time_angle)[:, None, :]
    cos_space = jnp.cos(space_angle)[:, None, :]
    sin_space = jnp.sin(space_angle)[:, None, :]
    first_part = values[:, :, :time_pairs]
    second_part = values[:, :, time_pairs : 2 * time_pairs]
    third_part = values[:, :, 2 * time_pairs : 2 * time_pairs + space_pairs]
    fourth_part = values[:, :, 2 * time_pairs + space_pairs :]
    return jnp.concatenate(
        [
            first_part * cos_time - second_part * sin_time,
            first_part * sin_time + second_part * cos_time,
            third_part * cos_space - fourth_part * sin_space,
            third_part * sin_space + fourth_part * cos_space,
        ],
        axis=-1,
    )


def token_positions(mask_block_frame, block_ids):
    count_blocks = mask_block_frame.shape[0]
    all_blocks = jnp.arange(count_blocks)
    same_frame = mask_block_frame[:, None] == mask_block_frame[None, :]
    first_block = jnp.min(jnp.where(same_frame, all_blocks[None, :], count_blocks), axis=1)
    inner_ids = jnp.arange(BLOCK)
    token_ids = block_ids[:, None] * BLOCK + inner_ids[None, :]
    frame_pos = (
        jnp.broadcast_to(mask_block_frame[block_ids][:, None], token_ids.shape)
        .reshape(-1)
        .astype(jnp.float32)
    )
    place = (token_ids - first_block[block_ids][:, None] * BLOCK).reshape(-1).astype(jnp.float32)
    return (frame_pos, place)


def body(
    tokens,
    mask_block_frame,
    attended_key_blocks,
    frozen_query_key_value,
    query_key_value_down_weight,
    query_key_value_up_weight,
    frozen_output_weight,
    output_down_weight,
    output_up_weight,
):
    tok_rows = tokens.shape[0]
    blocks_here = tok_rows // BLOCK
    local_width = frozen_output_weight.shape[0]
    heads_here = local_width // HEAD_SIZE
    adapter_rank_width = output_up_weight.shape[0]
    listed = attended_key_blocks.shape[1]
    weights_flat = frozen_query_key_value.reshape(MODEL_WIDTH, 3 * local_width)
    rank_segment = lax.all_gather(tokens, "head", axis=1, tiled=True)
    projected_rows = jnp.dot(rank_segment, weights_flat, preferred_element_type=jnp.float32)
    adapter_output_sum = jnp.dot(
        rank_segment, query_key_value_down_weight, preferred_element_type=jnp.float32
    )
    adapter_query_key_value = adapter_output_sum.astype(jnp.bfloat16).reshape(
        tok_rows, 3, adapter_rank_width
    )
    projected_rows = projected_rows.reshape(tok_rows, 3, local_width) + jnp.einsum(
        "ngc,cgz->ngz",
        adapter_query_key_value,
        query_key_value_up_weight,
        preferred_element_type=jnp.float32,
    )
    frame_index = lax.axis_index("frame")
    block_ids = frame_index * blocks_here + jnp.arange(blocks_here, dtype=jnp.int32)
    frame_pos, place = token_positions(mask_block_frame, block_ids)
    queries = rotate_pairs(
        projected_rows[:, 0].reshape(tok_rows, heads_here, HEAD_SIZE), frame_pos, place
    ).astype(jnp.bfloat16)
    keys = rotate_pairs(
        projected_rows[:, 1].reshape(tok_rows, heads_here, HEAD_SIZE), frame_pos, place
    ).astype(jnp.bfloat16)
    key_tiles = keys.reshape(blocks_here, BLOCK, local_width)
    value_tiles = projected_rows[:, 2].astype(jnp.bfloat16).reshape(blocks_here, BLOCK, local_width)
    my_lists = lax.dynamic_slice_in_dim(
        attended_key_blocks, frame_index * blocks_here, blocks_here, 0
    )
    pool_keys, pool_values = (
        lax.all_gather(key_tiles, "frame", axis=0, tiled=True),
        lax.all_gather(value_tiles, "frame", axis=0, tiled=True),
    )
    chosen_keys = pool_keys[my_lists].reshape(blocks_here, listed * BLOCK, heads_here, HEAD_SIZE)
    chosen_values = pool_values[my_lists].reshape(
        blocks_here, listed * BLOCK, heads_here, HEAD_SIZE
    )
    query_tiles = queries.reshape(blocks_here, BLOCK, heads_here, HEAD_SIZE)
    scores = jnp.einsum(
        "nqhd,nkhd->nhqk", query_tiles, chosen_keys, preferred_element_type=jnp.float32
    ) / math.sqrt(HEAD_SIZE)
    row_max = jnp.max(scores, axis=-1, keepdims=True)
    powers = jnp.exp(scores - row_max)
    probs = (powers / jnp.sum(powers, axis=-1, keepdims=True)).astype(jnp.bfloat16)
    attention_result = jnp.einsum(
        "nhqk,nkhd->nqhd", probs, chosen_values, preferred_element_type=jnp.float32
    ).astype(jnp.bfloat16)
    attention_result = attention_result.reshape(tok_rows, local_width)
    adapter_output = lax.psum(
        jnp.dot(attention_result, output_down_weight, preferred_element_type=jnp.float32).astype(
            jnp.bfloat16
        ),
        "head",
    )
    partial_value = jnp.dot(
        attention_result, frozen_output_weight, preferred_element_type=jnp.float32
    )
    frozen_output = lax.psum_scatter(
        partial_value.astype(jnp.bfloat16), "head", scatter_dimension=1, tiled=True
    ).astype(jnp.float32)
    return (
        frozen_output
        + jnp.dot(adapter_output, output_up_weight, preferred_element_type=jnp.float32)
    ).astype(jnp.bfloat16)


def solution(mesh):
    return jax.shard_map(
        body,
        mesh=mesh,
        in_specs=(
            P("frame", "head"),
            P(),
            P(),
            P(None, None, "head"),
            P(),
            P(None, None, "head"),
            P("head", None),
            P("head", None),
            P(None, "head"),
        ),
        out_specs=P("frame", "head"),
        check_vma=False,
    )
```

profile of v0, /device:TPU:0, one launch (start us, length us, event | category | flops | bytes accessed | tf_op | source)
XLA Modules:
  0.0 407.3 jit_solution(18228735309528296065)
XLA Ops:
  6.5 0.7 all-gather.4.cloned.1.call-update
  7.3 1.3 gather_fusion.1
  8.6 0.9 select_reduce_fusion
  9.6 0.6 gather_fusion.2
  10.2 16.2 %copy.37 = bf16[5120,3,384]{0,2,1:T(8,128)(2,1)} copy(bf16[5120,3,384]{2,0,1:T(8,128)(2,1)} %param.12) | data formatting | bytes 23592960 | tf_op args[3]
  26.9 0.6 multiply_cosine_fusion
  27.5 31.6 %all-gather.4.cloned.1.call-done = bf16[768,5120]{1,0:T(8,128)(2,1)} async-done(((bf16[768,640]{1,0:T(8,128)(2,1)}), bf16[768,5120]{1,0:T(8,128)(2,1)}) %all-gather.4.cloned.1.call-update) | async-done | bytes 7864336 | tf_op jit(solution)/shard_map/all_gather | solution.py:72
  59.2 6.1 %convolution_convert_fusion.1 = bf16[768,192]{0,1:T(8,128)(2,1)S(1)} fusion(bf16[768,5120]{1,0:T(8,128)(2,1)} %all-gather.4.cloned.1.call-done, bf16[5120,192]{0,1:T(8,128)(2,1)S(1)} %copy-done), kind=kOutput, calls=%fused_computation.22 | convolution fusion | flops 1510096896 | bytes 10125312 | tf_op jit(solution)/shard_map/dot_general | solution.py:74
  65.3 0.7 fusion.38
  66.0 13.3 %bitcast_add_fusion = f32[768,3,384]{0,2,1:T(8,128)S(1)} fusion(f32[3,768,384]{1,2,0:T(8,128)S(1)} %fusion.38, bf16[5120,3,384]{0,2,1:T(8,128)(2,1)S(1)} %copy-done.2, bf16[768,5120]{1,0:T(8,128)(2,1)} %all-gather.4.cloned.1.call-done), kind=kOutput, calls=%fused_computation.18 | convolution fusion | flops 9060581376 | bytes 26738688 | tf_op jit(solution)/shard_map/dot_general | solution.py:73
  80.0 1.1 copy-done.3
  81.2 0.7 convert_element_type.81
  81.9 1.3 copy.45
  83.2 1.3 slice.81
  84.5 1.1 copy.38
  88.5 70.3 %all-gather.8.cloned.1.call-done = bf16[96,128,384]{2,1,0:T(8,128)(2,1)} async-done(((bf16[6,128,384]{2,1,0:T(8,128)(2,1)}), bf16[96,128,384]{2,1,0:T(8,128)(2,1)}) %all-gather.8.cloned.1.call-update) | async-done | bytes 9437200 | tf_op jit(solution)/shard_map/all_gather | solution.py:101
  158.8 7.7 %gather_fusion.3 = bf16[60,128,384]{2,1,0:T(8,128)(2,1)} fusion(bf16[96,128,384]{2,1,0:T(8,128)(2,1)} %all-gather.8.cloned.1.call-done, s32[1024]{0:T(1024)S(1)} %pad_clamp_fusion.1), kind=kCustom, calls=%fused_computation.3 | custom fusion | bytes 11796720 | tf_op jit(solution)/shard_map/gather | solution.py:104
  166.5 15.9 %reshape.243 = bf16[6,1280,3,128]{3,2,1,0:T(4,128)(2,1)} reshape(bf16[60,128,384]{2,1,0:T(8,128)(2,1)} %gather_fusion.3) | data formatting | bytes 11796480 | tf_op jit(solution)/shard_map/reshape | solution.py:104
  182.4 9.4 %fusion.7 = f32[6,3,128,1280]{3,2,1,0:T(8,128)} fusion(bf16[6,1280,3,128]{3,2,1,0:T(4,128)(2,1)} %reshape.243, bf16[6,128,3,42]{3,1,2,0:T(8,128)(2,1)S(1)} %copy.44, bf16[6,128,3,42]{3,1,2,0:T(8,128)(2,1)S(1)} %copy.43, bf16[6,128,3,22]{3,1,2,0:T(8,128)(2,1)S(1)} %copy.42, bf16[6,128,3,22]{3,1,2,0:T(8,128)(2,1)S(1)} %copy.41), kind=kOutput, calls=%fused_computation.13 | convolution fusion | flops 757334016 | bytes 18284544 | tf_op jit(solution)/shard_map/nqhd,nkhd->nhqk/dot_general | solution.py:109
  191.8 15.6 %fusion.37 = (f32[6,3,128]{2,1,0:T(4,128)S(1)}, f32[6,3,128,1280]{3,2,1,0:T(8,128)}) fusion(f32[6,3,128,1280]{3,2,1,0:T(8,128)} %fusion.7), kind=kOutput, calls=%fused_computation.64 | output fusion | flops 11797759 | bytes 23602176 | tf_op jit(solution)/shard_map/sub | solution.py:113
  207.4 28.7 %all-gather.6.cloned.1.call-done = bf16[96,128,384]{2,1,0:T(8,128)(2,1)} async-done(((bf16[6,128,384]{2,1,0:T(8,128)(2,1)}), bf16[96,128,384]{2,1,0:T(8,128)(2,1)}) %all-gather.6.cloned.1.call-update) | async-done | bytes 9437200 | tf_op jit(solution)/shard_map/all_gather | solution.py:102
  236.1 7.8 %gather_fusion = bf16[60,128,384]{2,1,0:T(8,128)(2,1)} fusion(bf16[96,128,384]{2,1,0:T(8,128)(2,1)} %all-gather.6.cloned.1.call-done, s32[1024]{0:T(1024)S(1)} %pad_clamp_fusion.1), kind=kCustom, calls=%fused_computation | custom fusion | bytes 11796720 | tf_op jit(solution)/shard_map/gather | solution.py:105
  243.9 15.8 %reshape.242 = bf16[6,1280,3,128]{3,2,1,0:T(4,128)(2,1)} reshape(bf16[60,128,384]{2,1,0:T(8,128)(2,1)} %gather_fusion) | data formatting | bytes 11796480 | tf_op jit(solution)/shard_map/reshape | solution.py:105
  259.7 9.2 %fusion.19 = bf16[6,128,3,128]{1,3,2,0:T(8,128)(2,1)S(1)} fusion(f32[6,3,128,1280]{3,2,1,0:T(8,128)} %get-tuple-element.24, f32[6,3,128]{2,1,0:T(4,128)S(1)} %get-tuple-element.23, bf16[6,1280,3,128]{3,2,1,0:T(4,128)(2,1)} %reshape.242), kind=kOutput, calls=%fused_computation.21 | convolution fusion | flops 761167872 | bytes 18293760 | tf_op jit(solution)/shard_map/nhqk,nkhd->nqhd/dot_general | solution.py:115
  269.3 8.8 %convolution_convert_fusion = bf16[768,5120]{1,0:T(8,128)(2,1)} fusion(bf16[384,5120]{1,0:T(8,128)(2,1)} %param.15, bf16[48,8,6,128]{3,2,1,0:T(8,128)(2,1)S(1)} %bitcast.62), kind=kOutput, calls=%fused_computation.11 | convolution fusion | flops 3023831040 | bytes 12386304 | tf_op jit(solution)/shard_map/dot_general | solution.py:125
  278.1 10.6 %copy.54 = bf16[768,5120]{0,1:T(8,128)(2,1)} copy(bf16[768,5120]{1,0:T(8,128)(2,1)} %convolution_convert_fusion) | data formatting | bytes 15728640
  288.9 0.7 copy-done.6
  289.6 0.9 convolution_convert_fusion.2
  290.5 48.4 %reduce-scatter.4.cloned.1.call-done = bf16[640,768]{1,0:T(8,128)(2,1)} async-done(((bf16[5120,768]{1,0:T(8,128)(2,1)}), bf16[640,768]{1,0:T(8,128)(2,1)}) %reduce-scatter.4.cloned.1.call-update) | async-done | bytes 983056
  338.9 1.5 copy.55
  340.4 58.1 %all-reduce.2.cloned.1.call-done = bf16[768,64]{0,1:T(8,128)(2,1)} async-done(((bf16[768,64]{0,1:T(8,128)(2,1)}), bf16[768,64]{0,1:T(8,128)(2,1)}) %all-reduce.2.cloned.1.call-update) | async-done | bytes 98320 | tf_op jit(solution)/shard_map/psum | solution.py:119
  398.5 2.3 add_convert_fusion
  (49 shorter events, 4.8 us)
Async XLA Ops:
  6.5 52.6 %copy-start = (bf16[5120,192]{0,1:T(8,128)(2,1)S(1)}, bf16[5120,192]{0,1:T(8,128)(2,1)}, u32[]{:S(2)}) copy-start(bf16[5120,192]{0,1:T(8,128)(2,1)} %param.13) | copy-start | bytes 5898244
  6.5 52.6 %all-gather.4.cloned.1.call-start = ((), (), s32[]{:S(2)}) async-start(), calls=%async_computation.1 | async-start | bytes 8847360 | tf_op jit(solution)/shard_map/all_gather | solution.py:72
  7.3 151.5 %all-gather.8.cloned.1.call-start = ((), (), s32[]{:S(2)}) async-start(), calls=%async_computation.3 | async-start | bytes 10027008 | tf_op jit(solution)/shard_map/all_gather | solution.py:101
  27.5 37.8 %copy-start.4 = (bf16[64,3,384]{2,0,1:T(8,128)(2,1)S(1)}, bf16[64,3,384]{2,0,1:T(8,128)(2,1)}, u32[]{:S(2)}) copy-start(bf16[64,3,384]{2,0,1:T(8,128)(2,1)} %param.14) | copy-start | bytes 442372
  59.2 6.8 %copy-start.2 = (bf16[5120,3,384]{0,2,1:T(8,128)(2,1)S(1)}, bf16[5120,3,384]{0,2,1:T(8,128)(2,1)}, u32[]{:S(2)}) copy-start(bf16[5120,3,384]{0,2,1:T(8,128)(2,1)} %copy.37) | copy-start | bytes 35389444
  79.3 1.7 copy-start.3
  79.5 6.4 %copy-start.7 = (s32[96,10]{0,1:T(8,128)S(1)}, s32[96,10]{0,1:T(8,128)}, u32[]{:S(2)}) copy-start(s32[96,10]{0,1:T(8,128)} %param.11) | copy-start | bytes 11524
  83.1 152.9 %all-gather.6.cloned.1.call-start = ((), (), s32[]{:S(2)}) async-start(), calls=%async_computation.2 | async-start | bytes 10027008 | tf_op jit(solution)/shard_map/all_gather | solution.py:102
  85.6 253.2 %reduce-scatter.4.cloned.1.call-start = ((), (), s32[]{:S(2)}) async-start(), calls=%async_computation.5 | async-start | bytes 8847360
  288.8 0.8 copy-start.6
  288.8 109.7 %copy-start.5 = (bf16[64,640]{1,0:T(8,128)(2,1)S(1)}, bf16[64,640]{1,0:T(8,128)(2,1)}, u32[]{:S(2)}) copy-start(bf16[64,640]{1,0:T(8,128)(2,1)} %param.17) | copy-start | bytes 245764
  288.8 112.0 %copy-start.1 = (bf16[5120,192]{0,1:T(8,128)(2,1)S(1)}, bf16[5120,192]{0,1:T(8,128)(2,1)}, u32[]{:S(2)}) copy-start(bf16[5120,192]{0,1:T(8,128)(2,1)} %param.13) | copy-start | bytes 5898244
  288.8 109.7 %all-reduce.2.cloned.1.call-start = ((), (), s32[]{:S(2)}) async-start(), calls=%async_computation.4 | async-start | bytes 196608 | tf_op jit(solution)/shard_map/psum | solution.py:119
Sparse Core Ops, SparseCore 0:
  9.0 50.0 all-gather.3
  83.3 75.4 all-gather.7
  160.9 75.1 all-gather.5
  288.9 49.8 reduce-scatter.3
  341.0 57.4 all-reduce.1
where the time goes:
time: 409 us; the launch traced here: 407 us
  waiting for transfers between devices  238 us (58%)
  local copies, waits for them, and re-layouts  86.9 us (21%)
  matrix products  50.6 us (12%)
  other arithmetic  18.3 us (4%)
  between operations  13.3 us (3%)
    all_gather x1, waiting for transfers between devices, body(): lax.all_gather(key_tiles, 'frame', axis=0, tiled=True)  70.3 us
    psum x1, waiting for transfers between devices, body(): lax.psum(jnp.dot(attention_result, output_down_weight, preferred_element_...  58.1 us
    unnamed x6, waiting for transfers between devices  49.2 us
    all_gather x1, waiting for transfers between devices, body(): rank_segment = lax.all_gather(tokens, 'head', axis=1, tiled=True)  31.6 us
    unnamed x19, local copies, waits for them, and re-layouts  30.2 us
    all_gather x1, waiting for transfers between devices, body(): lax.all_gather(value_tiles, 'frame', axis=0, tiled=True)  28.7 us
    reshape x1, local copies, waits for them, and re-layouts, body(): pool_keys[my_lists]  15.9 us
    reshape x1, local copies, waits for them, and re-layouts, body(): pool_values[my_lists]  15.8 us
  transfers between devices with their start and end apart: 5, of which 5 were waited for; matrix products, arithmetic and copies ran while one was open for 19% of the time, Pallas kernels for 0%

commit v1 on v0

--- a/solution.py
+++ b/solution.py
@@ -116,11 +116,14 @@
         "nhqk,nkhd->nqhd", probs, chosen_values, preferred_element_type=jnp.float32
     ).astype(jnp.bfloat16)
     attention_result = attention_result.reshape(tok_rows, local_width)
-    adapter_output = lax.psum(
-        jnp.dot(attention_result, output_down_weight, preferred_element_type=jnp.float32).astype(
-            jnp.bfloat16
+    adapter_output = jnp.sum(
+        lax.all_gather(
+            jnp.dot(
+                attention_result, output_down_weight, preferred_element_type=jnp.float32
+            ).astype(jnp.bfloat16),
+            "head",
         ),
-        "head",
+        axis=0,
     )
     partial_value = jnp.dot(
         attention_result, frozen_output_weight, preferred_element_type=jnp.float32

time: 409 us -> 351 us (0.86)
  waiting for transfers between devices: 238 us -> 166 us
  blocking collectives: 0 us -> 14.6 us
    psum x1 -> x0, waiting for transfers between devices: 58.1 us -> none  [body(): lax.psum(jnp.dot(attention_result, output_down_weight, preferred_element_...]
    all_gather x0 -> x1, blocking collectives: none -> 14.6 us  [body(): lax.all_gather(jnp.dot(attention_result, output_down_weight, preferred_el...]
    unnamed x6 -> x5, waiting for transfers between devices: 49.2 us -> 35.5 us
    unnamed x19 -> x20, local copies, waits for them, and re-layouts: 30.2 us -> 30.3 us
  transfers between devices with their start and end apart: 5 -> 4, of which waited for: 5 -> 4; matrix products, arithmetic and copies ran while one was open for 19% -> 21% of each run, Pallas kernels for 0% -> 0%
where the time goes in v1:
time: 351 us; the launch traced here: 349 us
  waiting for transfers between devices  166 us (47%)
  local copies, waits for them, and re-layouts  87 us (25%)
  matrix products  49.1 us (14%)
  other arithmetic  18.9 us (5%)
  blocking collectives  14.6 us (4%)
  between operations  13.4 us (4%)
    all_gather x1, waiting for transfers between devices, body(): lax.all_gather(key_tiles, 'frame', axis=0, tiled=True)  70.2 us
    unnamed x5, waiting for transfers between devices  35.5 us
    all_gather x1, waiting for transfers between devices, body(): rank_segment = lax.all_gather(tokens, 'head', axis=1, tiled=True)  31.7 us
    unnamed x20, local copies, waits for them, and re-layouts  30.3 us
    all_gather x1, waiting for transfers between devices, body(): lax.all_gather(value_tiles, 'frame', axis=0, tiled=True)  28.7 us
    reshape x1, local copies, waits for them, and re-layouts, body(): pool_keys[my_lists]  15.9 us
    reshape x1, local copies, waits for them, and re-layouts, body(): pool_values[my_lists]  15.8 us
    sub x1, other arithmetic, body(): powers = jnp.exp(scores - row_max)  15.6 us
  transfers between devices with their start and end apart: 4, of which 4 were waited for; matrix products, arithmetic and copies ran while one was open for 21% of the time, Pallas kernels for 0%

profile of v1, /device:TPU:0, one launch (start us, length us, event | category | flops | bytes accessed | tf_op | source)
XLA Modules:
  0.0 349.4 jit_solution(8704891268743575743)
XLA Ops:
  6.5 0.7 all-gather.5.cloned.1.call-update
  7.3 1.3 gather_fusion.1
  8.6 0.9 select_reduce_fusion
  9.6 0.6 gather_fusion.2
  10.2 16.1 %copy.37 = bf16[5120,3,384]{0,2,1:T(8,128)(2,1)} copy(bf16[5120,3,384]{2,0,1:T(8,128)(2,1)} %param.12) | data formatting | bytes 23592960 | tf_op args[3]
  26.8 0.6 multiply_cosine_fusion
  27.4 31.7 %all-gather.5.cloned.1.call-done = bf16[768,5120]{1,0:T(8,128)(2,1)} async-done(((bf16[768,640]{1,0:T(8,128)(2,1)}), bf16[768,5120]{1,0:T(8,128)(2,1)}) %all-gather.5.cloned.1.call-update) | async-done | bytes 7864336 | tf_op jit(solution)/shard_map/all_gather | solution.py:72
  59.2 6.1 %convolution_convert_fusion.1 = bf16[768,192]{0,1:T(8,128)(2,1)S(1)} fusion(bf16[768,5120]{1,0:T(8,128)(2,1)} %all-gather.5.cloned.1.call-done, bf16[5120,192]{0,1:T(8,128)(2,1)S(1)} %copy-done), kind=kOutput, calls=%fused_computation.22 | convolution fusion | flops 1510096896 | bytes 10125312 | tf_op jit(solution)/shard_map/dot_general | solution.py:74
  65.3 0.7 fusion.38
  66.0 13.3 %bitcast_add_fusion = f32[768,3,384]{0,2,1:T(8,128)S(1)} fusion(f32[3,768,384]{1,2,0:T(8,128)S(1)} %fusion.38, bf16[5120,3,384]{0,2,1:T(8,128)(2,1)S(1)} %copy-done.2, bf16[768,5120]{1,0:T(8,128)(2,1)} %all-gather.5.cloned.1.call-done), kind=kOutput, calls=%fused_computation.18 | convolution fusion | flops 9060581376 | bytes 26738688 | tf_op jit(solution)/shard_map/dot_general | solution.py:73
  80.0 1.1 copy-done.3
  81.2 0.7 convert_element_type.83
  81.9 1.3 copy.45
  83.2 1.3 slice.81
  84.5 1.1 copy.38
  88.5 70.2 %all-gather.9.cloned.1.call-done = bf16[96,128,384]{2,1,0:T(8,128)(2,1)} async-done(((bf16[6,128,384]{2,1,0:T(8,128)(2,1)}), bf16[96,128,384]{2,1,0:T(8,128)(2,1)}) %all-gather.9.cloned.1.call-update) | async-done | bytes 9437200 | tf_op jit(solution)/shard_map/all_gather | solution.py:101
  158.8 7.7 %gather_fusion.3 = bf16[60,128,384]{2,1,0:T(8,128)(2,1)} fusion(bf16[96,128,384]{2,1,0:T(8,128)(2,1)} %all-gather.9.cloned.1.call-done, s32[1024]{0:T(1024)S(1)} %pad_clamp_fusion.1), kind=kCustom, calls=%fused_computation.3 | custom fusion | bytes 11796720 | tf_op jit(solution)/shard_map/gather | solution.py:104
  166.5 15.9 %reshape.244 = bf16[6,1280,3,128]{3,2,1,0:T(4,128)(2,1)} reshape(bf16[60,128,384]{2,1,0:T(8,128)(2,1)} %gather_fusion.3) | data formatting | bytes 11796480 | tf_op jit(solution)/shard_map/reshape | solution.py:104
  182.4 9.4 %fusion.7 = f32[6,3,128,1280]{3,2,1,0:T(8,128)} fusion(bf16[6,1280,3,128]{3,2,1,0:T(4,128)(2,1)} %reshape.244, bf16[6,128,3,42]{3,1,2,0:T(8,128)(2,1)S(1)} %copy.44, bf16[6,128,3,42]{3,1,2,0:T(8,128)(2,1)S(1)} %copy.43, bf16[6,128,3,22]{3,1,2,0:T(8,128)(2,1)S(1)} %copy.42, bf16[6,128,3,22]{3,1,2,0:T(8,128)(2,1)S(1)} %copy.41), kind=kOutput, calls=%fused_computation.13 | convolution fusion | flops 757334016 | bytes 18284544 | tf_op jit(solution)/shard_map/nqhd,nkhd->nhqk/dot_general | solution.py:109
  191.7 15.6 %fusion.37 = (f32[6,3,128]{2,1,0:T(4,128)S(1)}, f32[6,3,128,1280]{3,2,1,0:T(8,128)}) fusion(f32[6,3,128,1280]{3,2,1,0:T(8,128)} %fusion.7), kind=kOutput, calls=%fused_computation.65 | output fusion | flops 11797759 | bytes 23602176 | tf_op jit(solution)/shard_map/sub | solution.py:113
  207.4 28.7 %all-gather.7.cloned.1.call-done = bf16[96,128,384]{2,1,0:T(8,128)(2,1)} async-done(((bf16[6,128,384]{2,1,0:T(8,128)(2,1)}), bf16[96,128,384]{2,1,0:T(8,128)(2,1)}) %all-gather.7.cloned.1.call-update) | async-done | bytes 9437200 | tf_op jit(solution)/shard_map/all_gather | solution.py:102
  236.1 7.8 %gather_fusion = bf16[60,128,384]{2,1,0:T(8,128)(2,1)} fusion(bf16[96,128,384]{2,1,0:T(8,128)(2,1)} %all-gather.7.cloned.1.call-done, s32[1024]{0:T(1024)S(1)} %pad_clamp_fusion.1), kind=kCustom, calls=%fused_computation | custom fusion | bytes 11796720 | tf_op jit(solution)/shard_map/gather | solution.py:105
  243.9 15.8 %reshape.243 = bf16[6,1280,3,128]{3,2,1,0:T(4,128)(2,1)} reshape(bf16[60,128,384]{2,1,0:T(8,128)(2,1)} %gather_fusion) | data formatting | bytes 11796480 | tf_op jit(solution)/shard_map/reshape | solution.py:105
  259.7 9.2 %fusion.19 = bf16[6,128,3,128]{1,3,2,0:T(8,128)(2,1)S(1)} fusion(f32[6,3,128,1280]{3,2,1,0:T(8,128)} %get-tuple-element.24, f32[6,3,128]{2,1,0:T(4,128)S(1)} %get-tuple-element.23, bf16[6,1280,3,128]{3,2,1,0:T(4,128)(2,1)} %reshape.243), kind=kOutput, calls=%fused_computation.21 | convolution fusion | flops 761167872 | bytes 18293760 | tf_op jit(solution)/shard_map/nhqk,nkhd->nqhd/dot_general | solution.py:115
  269.3 8.8 %convolution_convert_fusion = bf16[768,5120]{1,0:T(8,128)(2,1)} fusion(bf16[384,5120]{1,0:T(8,128)(2,1)} %param.15, bf16[48,8,6,128]{3,2,1,0:T(8,128)(2,1)S(1)} %bitcast.68), kind=kOutput, calls=%fused_computation.11 | convolution fusion | flops 3023831040 | bytes 12386304 | tf_op jit(solution)/shard_map/dot_general | solution.py:128
  278.2 10.7 %copy.54 = bf16[768,5120]{0,1:T(8,128)(2,1)} copy(bf16[768,5120]{1,0:T(8,128)(2,1)} %convolution_convert_fusion) | data formatting | bytes 15728640
  288.8 0.8 copy-done.6
  289.8 14.6 %all-gather = bf16[6144,64]{0,1:T(8,128)(2,1)S(1)} all-gather(bf16[768,64]{0,1:T(8,128)(2,1)S(1)} %convolution_convert_fusion.2), channel_id=2, replica_groups=mesh['frame'=16,'head'=8] {'head'}, dimensions={0}, use_global_device_ids=true | all-gather | bytes 884736 | tf_op jit(solution)/shard_map/all_gather | solution.py:120
  304.6 0.6 bitcast_reduce_fusion
  305.2 34.7 %reduce-scatter.4.cloned.1.call-done = bf16[640,768]{1,0:T(8,128)(2,1)} async-done(((bf16[5120,768]{1,0:T(8,128)(2,1)}), bf16[640,768]{1,0:T(8,128)(2,1)}) %reduce-scatter.4.cloned.1.call-update) | async-done | bytes 983056
  339.9 1.5 copy.55
  341.4 1.4 add_convert_fusion
  (49 shorter events, 5.1 us)
Async XLA Ops:
  6.5 52.6 %copy-start = (bf16[5120,192]{0,1:T(8,128)(2,1)S(1)}, bf16[5120,192]{0,1:T(8,128)(2,1)}, u32[]{:S(2)}) copy-start(bf16[5120,192]{0,1:T(8,128)(2,1)} %param.13) | copy-start | bytes 5898244
  6.5 52.6 %all-gather.5.cloned.1.call-start = ((), (), s32[]{:S(2)}) async-start(), calls=%async_computation.1 | async-start | bytes 8847360 | tf_op jit(solution)/shard_map/all_gather | solution.py:72
  7.3 151.5 %all-gather.9.cloned.1.call-start = ((), (), s32[]{:S(2)}) async-start(), calls=%async_computation.3 | async-start | bytes 10027008 | tf_op jit(solution)/shard_map/all_gather | solution.py:101
  27.4 37.9 %copy-start.4 = (bf16[64,3,384]{2,0,1:T(8,128)(2,1)S(1)}, bf16[64,3,384]{2,0,1:T(8,128)(2,1)}, u32[]{:S(2)}) copy-start(bf16[64,3,384]{2,0,1:T(8,128)(2,1)} %param.14) | copy-start | bytes 442372
  59.2 6.8 %copy-start.2 = (bf16[5120,3,384]{0,2,1:T(8,128)(2,1)S(1)}, bf16[5120,3,384]{0,2,1:T(8,128)(2,1)}, u32[]{:S(2)}) copy-start(bf16[5120,3,384]{0,2,1:T(8,128)(2,1)} %copy.37) | copy-start | bytes 35389444
  79.3 1.8 copy-start.3
  79.5 6.4 %copy-start.7 = (s32[96,10]{0,1:T(8,128)S(1)}, s32[96,10]{0,1:T(8,128)}, u32[]{:S(2)}) copy-start(s32[96,10]{0,1:T(8,128)} %param.11) | copy-start | bytes 11524
  83.2 152.9 %all-gather.7.cloned.1.call-start = ((), (), s32[]{:S(2)}) async-start(), calls=%async_computation.2 | async-start | bytes 10027008 | tf_op jit(solution)/shard_map/all_gather | solution.py:102
  85.6 254.2 %reduce-scatter.4.cloned.1.call-start = ((), (), s32[]{:S(2)}) async-start(), calls=%async_computation.4 | async-start | bytes 8847360
  288.8 0.8 copy-start.6
  288.8 52.6 %copy-start.5 = (bf16[64,640]{1,0:T(8,128)(2,1)S(1)}, bf16[64,640]{1,0:T(8,128)(2,1)}, u32[]{:S(2)}) copy-start(bf16[64,640]{1,0:T(8,128)(2,1)} %param.17) | copy-start | bytes 245764
  289.6 53.2 %copy-start.1 = (bf16[5120,192]{0,1:T(8,128)(2,1)S(1)}, bf16[5120,192]{0,1:T(8,128)(2,1)}, u32[]{:S(2)}) copy-start(bf16[5120,192]{0,1:T(8,128)(2,1)} %param.13) | copy-start | bytes 5898244
Sparse Core Ops, SparseCore 0:
  9.0 50.0 all-gather.4
  83.3 75.4 all-gather.8
  160.9 75.1 all-gather.6
  289.0 50.8 reduce-scatter.3
